TPU v7x, 32 devices: a whole 2x2x4 slice. The times are simulated.
32 devices in a mesh: row: 4 (over y, core), col: 8 (over z, x).
Axes of the slice: x: 2, y: 2, z: 4, core: 2. Of those that a mesh axis runs over, the one named last changes fastest.
Arguments:
- embeddings: float32 [32768, 1024], P(('row', 'col')), may hold values from -6 to 6
- neighbour_ids: int32 [64, 12], P(('row', 'col')), may hold values from 0 to 63, as said below
- start_vectors: float32 [32768, 64], P(('row', 'col')), may hold values from -15 to 15
Outputs:
- spectral_vectors: float32 [32768, 64], P(('row', 'col'))
Inputs may be any that keep to these rules, and one draw needn't show every extreme that they name: `neighbour_ids`: slot 0 of block b is b itself. The other slots of block b name distinct blocks other than b held by devices of the same row index whose col index differs from that of b's device by at most 2 cyclically, followed by padding slots that repeat b. Block b sits on device b // 2, with device index row * 8 + col.
All inputs are finite; a program needn't handle non-finite values.
Results may differ from a plain program's by a relative error of at most 0.005.
Values may be sent and summed in bfloat16 or wider, within the bound.
No kernel may reach another device: no remote copies, remote signals or barrier semaphores. Data moves between devices by JAX's collectives and lax.ppermute only.
A program may use at most 128 MiB of HBM per device.

v0:
```python
import math
import jax
import jax.numpy as jnp
from jax import lax
from jax.sharding import PartitionSpec as P

D = 1024
BS = 512
SLOTS = 12
REACH = 2
ITERS = 3
BLK_DEV = 2
SHARP = 8.0
EPSILON = 1e-06


def passed_along(shard, axis, by):
    count = lax.axis_size(axis)
    return lax.ppermute(shard, axis, [(i, (i + by) % count) for i in range(count)])


def unit_rows(points):
    rms_inverse = lax.rsqrt(jnp.mean(points * points, axis=-1, keepdims=True) + EPSILON)
    return (points * rms_inverse).astype(jnp.bfloat16)


def band_index(neighbour_ids, col_count, col_index):
    holder = neighbour_ids // BLK_DEV
    offset = (holder % col_count - col_index + col_count + REACH) % col_count
    return offset * BLK_DEV + neighbour_ids % BLK_DEV


def assemble(pieces):
    return jnp.concatenate([pieces[offset] for offset in range(-REACH, REACH + 1)], axis=0)


def point_band(normed):
    pieces = {0: normed}
    for offset in [shifted for shifted in range(-REACH, REACH + 1) if shifted != 0]:
        pieces[offset] = passed_along(normed, "col", -offset)
    return assemble(pieces)


def vector_band(scaled):
    pieces = {0: scaled}
    for offset in [shifted for shifted in range(-REACH, REACH + 1) if shifted != 0]:
        pieces[offset] = passed_along(scaled, "col", -offset)
    return assemble(pieces)


def orthonormal(image_rows, total_rows):
    gram_sum = lax.dot_general(
        image_rows,
        image_rows,
        (((0,), (0,)), ((), ())),
        precision=lax.Precision.HIGHEST,
        preferred_element_type=jnp.float32,
    )
    gram_sum = lax.psum(gram_sum, ("row", "col"))
    factor = jnp.linalg.cholesky(gram_sum)
    solved = lax.linalg.triangular_solve(
        factor, image_rows, left_side=False, lower=True, transpose_a=True
    )
    return solved * math.sqrt(total_rows)


def on_device(embeddings, neighbour_ids, start_vectors):
    col_count = lax.axis_size("col")
    col_index = lax.axis_index("col")
    device = lax.axis_index("row") * col_count + col_index
    total_rows = embeddings.shape[0] * lax.axis_size("row") * col_count
    normed = unit_rows(embeddings)
    point_rows = point_band(normed)
    own_ids = device * BLK_DEV + jnp.arange(BLK_DEV, dtype=jnp.int32)
    slot_ids = jnp.arange(SLOTS, dtype=jnp.int32)
    live_mask = ((slot_ids[None, :] == 0) | (neighbour_ids != own_ids[:, None])).astype(jnp.float32)
    position = band_index(neighbour_ids, col_count, col_index)
    candidates = (2 * REACH + 1) * BLK_DEV
    own_blocks = normed.reshape(BLK_DEV, BS, D)
    tile_list = []
    degree_list = []
    chosen = jnp.sum(
        (position[:, :, None] == jnp.arange(candidates, dtype=jnp.int32)[None, None, :]).astype(
            jnp.float32
        )
        * live_mask[:, :, None],
        axis=1,
    )
    for member in range(BLK_DEV):
        cosine = (
            lax.dot_general(
                own_blocks[member],
                point_rows,
                (((1,), (1,)), ((), ())),
                preferred_element_type=jnp.float32,
            )
            / D
        )
        affinity = (
            jnp.exp(SHARP * (cosine - 1.0)).reshape(BS, candidates, BS)
            * chosen[member][None, :, None]
        )
        degree_list.append(jnp.sum(affinity, axis=(1, 2)))
        tile_list.append(affinity.reshape(BS, candidates * BS).astype(jnp.bfloat16))
    inv_root = lax.rsqrt(jnp.stack(degree_list))
    vectors = start_vectors
    for iteration in range(ITERS):
        scaled = (vectors * inv_root.reshape(-1, 1)).astype(jnp.bfloat16)
        spread = vector_band(scaled)
        image_list = []
        for member in range(BLK_DEV):
            partial_rows = jnp.dot(tile_list[member], spread, preferred_element_type=jnp.float32)
            image_list.append(partial_rows * inv_root[member][:, None])
        image_rows = jnp.concatenate(image_list, axis=0)
        vectors = orthonormal(image_rows, total_rows)
    return vectors


def solution(mesh):
    in_specs = (P(("row", "col"), None), P(("row", "col"), None), P(("row", "col"), None))
    out_specs = P(("row", "col"), None)
    return jax.shard_map(
        on_device, mesh=mesh, in_specs=in_specs, out_specs=out_specs, check_vma=False
    )
```

profile of v0, /device:TPU:0, one launch (start us, length us, event | category | flops | bytes accessed | tf_op | source)
XLA Modules:
  0.0 388.7 jit_solution(13238385011617048183)
XLA Ops:
  9.6 3.2 collective-permute-start.2
  13.7 43.3 %collective-permute-done = bf16[1024,1024]{1,0:T(8,128)(2,1)} collective-permute-done((bf16[1024,1024]{1,0:T(8,128)(2,1)}, bf16[1024,1024]{1,0:T(8,128)(2,1)}, u32[]{:S(2)}, u32[]{:S(2)}) %collective-permute-start) | collective-permute-done | bytes 2097184 | tf_op jit(solution)/shard_map/ppermute | solution.py:19
  60.1 43.0 %collective-permute-done.1 = bf16[1024,1024]{1,0:T(8,128)(2,1)} collective-permute-done((bf16[1024,1024]{1,0:T(8,128)(2,1)}, bf16[1024,1024]{1,0:T(8,128)(2,1)}, u32[]{:S(2)}, u32[]{:S(2)}) %collective-permute-start.1) | collective-permute-done | bytes 2097184 | tf_op jit(solution)/shard_map/ppermute | solution.py:19
  103.1 3.1 constant_dynamic-update-slice_fusion.3
  107.8 3.2 constant_dynamic-update-slice_fusion.1
  111.0 34.9 %collective-permute-done.3 = bf16[1024,1024]{1,0:T(8,128)(2,1)S(1)} collective-permute-done((bf16[1024,1024]{1,0:T(8,128)(2,1)}, bf16[1024,1024]{1,0:T(8,128)(2,1)S(1)}, u32[]{:S(2)}, u32[]{:S(2)}) %collective-permute-start.3) | collective-permute-done | bytes 2097184 | tf_op jit(solution)/shard_map/ppermute | solution.py:19
  147.4 10.0 %fusion.45 = (f32[512]{0:T(512)S(1)}, bf16[512,5120]{1,0:T(8,128)(2,1)S(1)}) fusion(f32[5120]{0:T(1024)S(1)} %mul.152, bf16[5120,1024]{1,0:T(8,128)(2,1)} %constant_dynamic-update-slice_fusion, bf16[1024,1024]{1,0:T(8,128)(2,1)} %multiply_convert_fusion), kind=kOutput, calls=%fused_computation.114 | convolution fusion | flops 5384437248 | bytes 16799744 | tf_op jit(solution)/shard_map/dot_general | solution.py:91
  157.4 11.9 %fusion.44 = (f32[512]{0:T(512)S(1)}, bf16[512,5120]{1,0:T(8,128)(2,1)S(1)}) fusion(f32[5120]{0:T(1024)S(1)} %mul.158, bf16[5120,1024]{1,0:T(8,128)(2,1)} %constant_dynamic-update-slice_fusion, bf16[1024,1024]{1,0:T(8,128)(2,1)} %multiply_convert_fusion), kind=kOutput, calls=%fused_computation.113 | convolution fusion | flops 5384437248 | bytes 16799744 | tf_op jit(solution)/shard_map/dot_general | solution.py:91
  171.6 3.3 collective-permute-start.6
  174.8 10.5 %collective-permute-start.7 = (bf16[1024,64]{0,1:T(8,128)(2,1)S(1)}, bf16[1024,64]{0,1:T(8,128)(2,1)S(1)}, u32[]{:S(2)}, u32[]{:S(2)}) collective-permute-start(bf16[1024,64]{0,1:T(8,128)(2,1)S(1)} %multiply_convert_fusion.1), channel_id=1, source_target_pairs={{0,6},{1,7},{2,0},{3,1},{4,2},{5,3},{6,4},{7,5},{8,14},{9,15},{10,... | collective-permute-start | bytes 393224 | tf_op jit(solution)/shard_map/ppermute | solution.py:19
  192.9 39.6 %psum.21 = f32[64,64]{0,1:T(8,128)S(1)} all-reduce(f32[64,64]{0,1:T(8,128)S(1)} %fusion.9), channel_id=1, replica_groups=mesh['row'=4,'col'=8] {'row','col'}, use_global_device_ids=true, to_apply=%region_4.5 | all-reduce | flops 4096 | bytes 32768 | tf_op jit(solution)/shard_map/psum | solution.py:59
  232.6 5.8 %cholesky.59 = f32[64,64]{1,0:T(8,128)S(1)} custom-call(f32[64,64]{1,0:T(8,128)S(1)} %fusion.18), custom_call_target="Cholesky" | custom-call | tf_op jit(solution)/shard_map/jit(cholesky)/cholesky | solution.py:60
  239.8 4.9 %custom-call.7 = f32[1,64,64]{1,2,0:T(8,128)S(1)} custom-call(f32[1,64,64]{2,1,0:T(8,128)S(1)} %fusion.10), custom_call_target="InvertDiagBlocksLowerTriangular" | custom-call | tf_op jit(solution)/shard_map/triangular_solve/custom-call.0 | solution.py:61
  252.9 4.5 %collective-permute-done.9 = bf16[1024,64]{0,1:T(8,128)(2,1)S(1)} collective-permute-done((bf16[1024,64]{0,1:T(8,128)(2,1)S(1)}, bf16[1024,64]{0,1:T(8,128)(2,1)S(1)}, u32[]{:S(2)}, u32[]{:S(2)}) %collective-permute-start.9) | collective-permute-done | bytes 131104 | tf_op jit(solution)/shard_map/ppermute | solution.py:19
  257.5 4.2 %convolution_multiply_fusion.3 = f32[512,64]{0,1:T(8,128)S(1)} fusion(bf16[5120,64]{0,1:T(8,128)(2,1)S(1)} %constant_dynamic-update-slice_fusion.10, f32[512]{0:T(512)S(1)} %bitcast.68, bf16[512,5120]{1,0:T(8,128)(2,1)} %copy-done), kind=kOutput, calls=%fused_computation.15 | convolution fusion | flops 335577088 | bytes 6031360 | tf_op jit(solution)/shard_map/dot_general | solution.py:112
  263.8 38.8 %psum.22 = f32[64,64]{0,1:T(8,128)S(1)} all-reduce(f32[64,64]{0,1:T(8,128)S(1)} %fusion.8), channel_id=1, replica_groups=mesh['row'=4,'col'=8] {'row','col'}, use_global_device_ids=true, to_apply=%region_7.10 | all-reduce | flops 4096 | bytes 32768 | tf_op jit(solution)/shard_map/psum | solution.py:59
  302.7 5.8 %cholesky.70 = f32[64,64]{1,0:T(8,128)S(1)} custom-call(f32[64,64]{1,0:T(8,128)S(1)} %fusion.16), custom_call_target="Cholesky" | custom-call | tf_op jit(solution)/shard_map/jit(cholesky)/cholesky | solution.py:60
  309.9 4.9 %custom-call.8 = f32[1,64,64]{1,2,0:T(8,128)S(1)} custom-call(f32[1,64,64]{2,1,0:T(8,128)S(1)} %fusion.11), custom_call_target="InvertDiagBlocksLowerTriangular" | custom-call | tf_op jit(solution)/shard_map/triangular_solve/custom-call.0 | solution.py:61
  323.0 4.5 %collective-permute-done.13 = bf16[1024,64]{0,1:T(8,128)(2,1)S(1)} collective-permute-done((bf16[1024,64]{0,1:T(8,128)(2,1)S(1)}, bf16[1024,64]{0,1:T(8,128)(2,1)S(1)}, u32[]{:S(2)}, u32[]{:S(2)}) %collective-permute-start.13) | collective-permute-done | bytes 131104 | tf_op jit(solution)/shard_map/ppermute | solution.py:19
  327.6 4.2 %convolution_multiply_fusion.1 = f32[512,64]{0,1:T(8,128)S(1)} fusion(bf16[5120,64]{0,1:T(8,128)(2,1)S(1)} %constant_dynamic-update-slice_fusion.15, f32[512]{0:T(512)S(1)} %bitcast.69, bf16[512,5120]{1,0:T(8,128)(2,1)} %copy-done), kind=kOutput, calls=%fused_computation.13 | convolution fusion | flops 335577088 | bytes 6031360 | tf_op jit(solution)/shard_map/dot_general | solution.py:112
  331.8 4.2 %convolution_multiply_fusion = f32[512,64]{0,1:T(8,128)S(1)} fusion(bf16[5120,64]{0,1:T(8,128)(2,1)S(1)} %constant_dynamic-update-slice_fusion.15, f32[512]{0:T(512)S(1)} %bitcast.66, bf16[512,5120]{1,0:T(8,128)(2,1)} %copy-done.1), kind=kOutput, calls=%fused_computation.12 | convolution fusion | flops 335577088 | bytes 6031360 | tf_op jit(solution)/shard_map/dot_general | solution.py:112
  336.3 39.1 %psum.23 = f32[64,64]{0,1:T(8,128)S(1)} all-reduce(f32[64,64]{0,1:T(8,128)S(1)} %fusion.7), channel_id=1, replica_groups=mesh['row'=4,'col'=8] {'row','col'}, use_global_device_ids=true, to_apply=%region_8.11 | all-reduce | flops 4096 | bytes 32768 | tf_op jit(solution)/shard_map/psum | solution.py:59
  375.5 5.8 %cholesky.81 = f32[64,64]{1,0:T(8,128)S(1)} custom-call(f32[64,64]{1,0:T(8,128)S(1)} %fusion.14), custom_call_target="Cholesky" | custom-call | tf_op jit(solution)/shard_map/jit(cholesky)/cholesky | solution.py:60
  382.7 4.9 %custom-call.9 = f32[1,64,64]{1,2,0:T(8,128)S(1)} custom-call(f32[1,64,64]{2,1,0:T(8,128)S(1)} %fusion.12), custom_call_target="InvertDiagBlocksLowerTriangular" | custom-call | tf_op jit(solution)/shard_map/triangular_solve/custom-call.0 | solution.py:61
  (98 shorter events, 50.6 us)
Async XLA Ops:
  0.0 3.4 copy-start.3
  0.0 13.1 %copy-start.6 = (s32[2,12]{1,0:T(2,128)S(1)}, s32[2,12]{1,0:T(2,128)}, u32[]{:S(2)}) copy-start(s32[2,12]{1,0:T(2,128)} %param.7) | copy-start | bytes 292
  5.1 51.9 %collective-permute-start = (bf16[1024,1024]{1,0:T(8,128)(2,1)}, bf16[1024,1024]{1,0:T(8,128)(2,1)}, u32[]{:S(2)}, u32[]{:S(2)}) collective-permute-start(bf16[1024,1024]{1,0:T(8,128)(2,1)} %multiply_convert_fusion), channel_id=1, source_target_pairs={{0,2},{1,3},{2,4},{3,5},{4,6},{5,7},{6,0},{7,1},{8,10},{9,11},{10,... | collective-permute-start | bytes 6291464 | tf_op jit(solution)/shard_map/ppermute | solution.py:19
  8.1 94.9 %collective-permute-start.1 = (bf16[1024,1024]{1,0:T(8,128)(2,1)}, bf16[1024,1024]{1,0:T(8,128)(2,1)}, u32[]{:S(2)}, u32[]{:S(2)}) collective-permute-start(bf16[1024,1024]{1,0:T(8,128)(2,1)} %multiply_convert_fusion), channel_id=1, source_target_pairs={{0,1},{1,2},{2,3},{3,4},{4,5},{5,6},{6,7},{7,0},{8,9},{9,10},{10,1... | collective-permute-start | bytes 6291464 | tf_op jit(solution)/shard_map/ppermute | solution.py:19
  9.6 98.2 %collective-permute-start.2 = (bf16[1024,1024]{1,0:T(8,128)(2,1)}, bf16[1024,1024]{1,0:T(8,128)(2,1)}, u32[]{:S(2)}, u32[]{:S(2)}) collective-permute-start(bf16[1024,1024]{1,0:T(8,128)(2,1)} %multiply_convert_fusion), channel_id=1, source_target_pairs={{0,7},{1,0},{2,1},{3,2},{4,3},{5,4},{6,5},{7,6},{8,15},{9,8},{10,9... | collective-permute-start | bytes 6291464 | tf_op jit(solution)/shard_map/ppermute | solution.py:19
  12.9 133.0 %collective-permute-start.3 = (bf16[1024,1024]{1,0:T(8,128)(2,1)}, bf16[1024,1024]{1,0:T(8,128)(2,1)S(1)}, u32[]{:S(2)}, u32[]{:S(2)}) collective-permute-start(bf16[1024,1024]{1,0:T(8,128)(2,1)} %multiply_convert_fusion), channel_id=1, source_target_pairs={{0,6},{1,7},{2,0},{3,1},{4,2},{5,3},{6,4},{7,5},{8,14},{9,15},{10,... | collective-permute-start | bytes 6291464 | tf_op jit(solution)/shard_map/ppermute | solution.py:19
  13.7 92.5 %copy-start.4 = (f32[1024,1024]{1,0:T(8,128)S(1)}, f32[1024,1024]{1,0:T(8,128)}, u32[]{:S(2)}) copy-start(f32[1024,1024]{1,0:T(8,128)} %param.6) | copy-start | bytes 12582916
  157.4 31.7 %copy-start = (bf16[512,5120]{1,0:T(8,128)(2,1)}, bf16[512,5120]{1,0:T(8,128)(2,1)S(1)}, u32[]{:S(2)}) copy-start(bf16[512,5120]{1,0:T(8,128)(2,1)S(1)} %get-tuple-element.16) | copy-start | bytes 15728644
  157.4 12.0 %copy-start.5 = (f32[1024,64]{0,1:T(8,128)S(1)}, f32[1024,64]{0,1:T(8,128)}, u32[]{:S(2)}) copy-start(f32[1024,64]{0,1:T(8,128)} %param.8) | copy-start | bytes 786436
  169.4 23.2 %copy-start.1 = (bf16[512,5120]{1,0:T(8,128)(2,1)}, bf16[512,5120]{1,0:T(8,128)(2,1)S(1)}, u32[]{:S(2)}) copy-start(bf16[512,5120]{1,0:T(8,128)(2,1)S(1)} %get-tuple-element.14) | copy-start | bytes 15728644
  169.4 15.8 %collective-permute-start.4 = (bf16[1024,64]{0,1:T(8,128)(2,1)S(1)}, bf16[1024,64]{0,1:T(8,128)(2,1)S(1)}, u32[]{:S(2)}, u32[]{:S(2)}) collective-permute-start(bf16[1024,64]{0,1:T(8,128)(2,1)S(1)} %multiply_convert_fusion.1), channel_id=1, source_target_pairs={{0,2},{1,3},{2,4},{3,5},{4,6},{5,7},{6,0},{7,1},{8,10},{9,11},{10,... | collective-permute-start | bytes 393224 | tf_op jit(solution)/shard_map/ppermute | solution.py:19
  170.1 15.2 %collective-permute-start.5 = (bf16[1024,64]{0,1:T(8,128)(2,1)S(1)}, bf16[1024,64]{0,1:T(8,128)(2,1)S(1)}, u32[]{:S(2)}, u32[]{:S(2)}) collective-permute-start(bf16[1024,64]{0,1:T(8,128)(2,1)S(1)} %multiply_convert_fusion.1), channel_id=1, source_target_pairs={{0,1},{1,2},{2,3},{3,4},{4,5},{5,6},{6,7},{7,0},{8,9},{9,10},{10,1... | collective-permute-start | bytes 393224 | tf_op jit(solution)/shard_map/ppermute | solution.py:19
  171.6 14.7 %collective-permute-start.6 = (bf16[1024,64]{0,1:T(8,128)(2,1)S(1)}, bf16[1024,64]{0,1:T(8,128)(2,1)S(1)}, u32[]{:S(2)}, u32[]{:S(2)}) collective-permute-start(bf16[1024,64]{0,1:T(8,128)(2,1)S(1)} %multiply_convert_fusion.1), channel_id=1, source_target_pairs={{0,7},{1,0},{2,1},{3,2},{4,3},{5,4},{6,5},{7,6},{8,15},{9,8},{10,9... | collective-permute-start | bytes 393224 | tf_op jit(solution)/shard_map/ppermute | solution.py:19
  174.8 14.3 %collective-permute-start.7 = (bf16[1024,64]{0,1:T(8,128)(2,1)S(1)}, bf16[1024,64]{0,1:T(8,128)(2,1)S(1)}, u32[]{:S(2)}, u32[]{:S(2)}) collective-permute-start(bf16[1024,64]{0,1:T(8,128)(2,1)S(1)} %multiply_convert_fusion.1), channel_id=1, source_target_pairs={{0,6},{1,7},{2,0},{3,1},{4,2},{5,3},{6,4},{7,5},{8,14},{9,15},{10,... | collective-permute-start | bytes 393224 | tf_op jit(solution)/shard_map/ppermute | solution.py:19
  244.7 17.0 %copy-start.2 = (bf16[512,5120]{1,0:T(8,128)(2,1)S(1)}, bf16[512,5120]{1,0:T(8,128)(2,1)}, u32[]{:S(2)}) copy-start(bf16[512,5120]{1,0:T(8,128)(2,1)} %copy-done.1) | copy-start | bytes 15728644
  245.1 7.7 %collective-permute-start.8 = (bf16[1024,64]{0,1:T(8,128)(2,1)S(1)}, bf16[1024,64]{0,1:T(8,128)(2,1)S(1)}, u32[]{:S(2)}, u32[]{:S(2)}) collective-permute-start(bf16[1024,64]{0,1:T(8,128)(2,1)S(1)} %fusion.3), channel_id=1, source_target_pairs={{0,2},{1,3},{2,4},{3,5},{4,6},{5,7},{6,0},{7,1},{8,10},{9,11},{10,... | collective-permute-start | bytes 393224 | tf_op jit(solution)/shard_map/ppermute | solution.py:19
  246.3 11.1 %collective-permute-start.9 = (bf16[1024,64]{0,1:T(8,128)(2,1)S(1)}, bf16[1024,64]{0,1:T(8,128)(2,1)S(1)}, u32[]{:S(2)}, u32[]{:S(2)}) collective-permute-start(bf16[1024,64]{0,1:T(8,128)(2,1)S(1)} %fusion.3), channel_id=1, source_target_pairs={{0,1},{1,2},{2,3},{3,4},{4,5},{5,6},{6,7},{7,0},{8,9},{9,10},{10,1... | collective-permute-start | bytes 393224 | tf_op jit(solution)/shard_map/ppermute | solution.py:19
  248.5 8.9 %collective-permute-start.10 = (bf16[1024,64]{0,1:T(8,128)(2,1)S(1)}, bf16[1024,64]{0,1:T(8,128)(2,1)S(1)}, u32[]{:S(2)}, u32[]{:S(2)}) collective-permute-start(bf16[1024,64]{0,1:T(8,128)(2,1)S(1)} %fusion.3), channel_id=1, source_target_pairs={{0,7},{1,0},{2,1},{3,2},{4,3},{5,4},{6,5},{7,6},{8,15},{9,8},{10,9... | collective-permute-start | bytes 393224 | tf_op jit(solution)/shard_map/ppermute | solution.py:19
  251.0 6.5 %collective-permute-start.11 = (bf16[1024,64]{0,1:T(8,128)(2,1)S(1)}, bf16[1024,64]{0,1:T(8,128)(2,1)S(1)}, u32[]{:S(2)}, u32[]{:S(2)}) collective-permute-start(bf16[1024,64]{0,1:T(8,128)(2,1)S(1)} %fusion.3), channel_id=1, source_target_pairs={{0,6},{1,7},{2,0},{3,1},{4,2},{5,3},{6,4},{7,5},{8,14},{9,15},{10,... | collective-permute-start | bytes 393224 | tf_op jit(solution)/shard_map/ppermute | solution.py:19
  315.2 7.7 %collective-permute-start.12 = (bf16[1024,64]{0,1:T(8,128)(2,1)S(1)}, bf16[1024,64]{0,1:T(8,128)(2,1)S(1)}, u32[]{:S(2)}, u32[]{:S(2)}) collective-permute-start(bf16[1024,64]{0,1:T(8,128)(2,1)S(1)} %fusion.4), channel_id=1, source_target_pairs={{0,2},{1,3},{2,4},{3,5},{4,6},{5,7},{6,0},{7,1},{8,10},{9,11},{10,... | collective-permute-start | bytes 393224 | tf_op jit(solution)/shard_map/ppermute | solution.py:19
  316.8 10.7 %collective-permute-start.13 = (bf16[1024,64]{0,1:T(8,128)(2,1)S(1)}, bf16[1024,64]{0,1:T(8,128)(2,1)S(1)}, u32[]{:S(2)}, u32[]{:S(2)}) collective-permute-start(bf16[1024,64]{0,1:T(8,128)(2,1)S(1)} %fusion.4), channel_id=1, source_target_pairs={{0,1},{1,2},{2,3},{3,4},{4,5},{5,6},{6,7},{7,0},{8,9},{9,10},{10,1... | collective-permute-start | bytes 393224 | tf_op jit(solution)/shard_map/ppermute | solution.py:19
  319.1 8.5 %collective-permute-start.14 = (bf16[1024,64]{0,1:T(8,128)(2,1)S(1)}, bf16[1024,64]{0,1:T(8,128)(2,1)S(1)}, u32[]{:S(2)}, u32[]{:S(2)}) collective-permute-start(bf16[1024,64]{0,1:T(8,128)(2,1)S(1)} %fusion.4), channel_id=1, source_target_pairs={{0,7},{1,0},{2,1},{3,2},{4,3},{5,4},{6,5},{7,6},{8,15},{9,8},{10,9... | collective-permute-start | bytes 393224 | tf_op jit(solution)/shard_map/ppermute | solution.py:19
  321.5 6.0 %collective-permute-start.15 = (bf16[1024,64]{0,1:T(8,128)(2,1)S(1)}, bf16[1024,64]{0,1:T(8,128)(2,1)S(1)}, u32[]{:S(2)}, u32[]{:S(2)}) collective-permute-start(bf16[1024,64]{0,1:T(8,128)(2,1)S(1)} %fusion.4), channel_id=1, source_target_pairs={{0,6},{1,7},{2,0},{3,1},{4,2},{5,3},{6,4},{7,5},{8,14},{9,15},{10,... | collective-permute-start | bytes 393224 | tf_op jit(solution)/shard_map/ppermute | solution.py:19
where the time goes:
time: 389 us
  waiting for transfers between devices  136 us (35%)
  blocking collectives  117 us (30%)
  matrix products  42.8 us (11%)
  other arithmetic  42.4 us (11%)
  starting transfers between devices  37.5 us (10%)
  local copies, waits for them, and re-layouts  12.3 us (3%)
    ppermute x16, waiting for transfers between devices, passed_along(): lax.ppermute(shard, axis, [(i, (i + by) % count) for i in range(count)])  136 us
    psum x3, blocking collectives, orthonormal(): gram_sum = lax.psum(gram_sum, ('row', 'col'))  117 us
    ppermute x16, starting transfers between devices, passed_along(): lax.ppermute(shard, axis, [(i, (i + by) % count) for i in range(count)])  37.5 us
    dot_general x2, matrix products, on_device(): lax.dot_general(own_blocks[member], point_rows, (((1,), (1,)), ((), ())),...  22 us
    another operation x9, other arithmetic, orthonormal(): factor = jnp.linalg.cholesky(gram_sum)  19.6 us
    dot_general x6, matrix products, on_device(): jnp.dot(tile_list[member], spread, preferred_element_type=jnp.float32)  17.7 us
    another operation x6, other arithmetic, orthonormal(): lax.linalg.triangular_solve(factor, image_rows, left_side=False, lower=Tr...  16.6 us
    unnamed x29, local copies, waits for them, and re-layouts  10.2 us
  transfers between devices with their start and end apart: 16, of which 9 were waited for; matrix products, arithmetic and copies ran while one was open for 3% of the time, Pallas kernels for 0%

commit v1 on v0

--- a/solution.py
+++ b/solution.py
@@ -56,7 +56,8 @@
         precision=lax.Precision.HIGHEST,
         preferred_element_type=jnp.float32,
     )
-    gram_sum = lax.psum(gram_sum, ("row", "col"))
+    for over in ("col", "row"):
+        gram_sum = lax.psum(gram_sum, over)
     factor = jnp.linalg.cholesky(gram_sum)
     solved = lax.linalg.triangular_solve(
         factor, image_rows, left_side=False, lower=True, transpose_a=True

time: 389 us -> 406 us (1.044)
  blocking collectives: 117 us -> 138 us
    psum x3 -> x6, blocking collectives: 117 us -> 138 us  [orthonormal(): gram_sum = lax.psum(gram_sum, over)]
  transfers between devices with their start and end apart: 16 -> 16, of which waited for: 9 -> 11; matrix products, arithmetic and copies ran while one was open for 3% -> 3% of each run, Pallas kernels for 0% -> 0%
where the time goes in v1:
time: 406 us
  blocking collectives  138 us (34%)
  waiting for transfers between devices  133 us (33%)
  matrix products  42.8 us (11%)
  other arithmetic  42.4 us (10%)
  starting transfers between devices  37.4 us (9%)
  local copies, waits for them, and re-layouts  12.3 us (3%)
    psum x6, blocking collectives, orthonormal(): gram_sum = lax.psum(gram_sum, over)  138 us
    ppermute x16, waiting for transfers between devices, passed_along(): lax.ppermute(shard, axis, [(i, (i + by) % count) for i in range(count)])  133 us
    ppermute x16, starting transfers between devices, passed_along(): lax.ppermute(shard, axis, [(i, (i + by) % count) for i in range(count)])  37.4 us
    dot_general x2, matrix products, on_device(): lax.dot_general(own_blocks[member], point_rows, (((1,), (1,)), ((), ())),...  22 us
    another operation x9, other arithmetic, orthonormal(): factor = jnp.linalg.cholesky(gram_sum)  19.6 us
    dot_general x6, matrix products, on_device(): jnp.dot(tile_list[member], spread, preferred_element_type=jnp.float32)  17.7 us
    another operation x6, other arithmetic, orthonormal(): lax.linalg.triangular_solve(factor, image_rows, left_side=False, lower=Tr...  16.6 us
    unnamed x29, local copies, waits for them, and re-layouts  10.2 us
  transfers between devices with their start and end apart: 16, of which 11 were waited for; matrix products, arithmetic and copies ran while one was open for 3% of the time, Pallas kernels for 0%

profile of v1, /device:TPU:0, one launch (start us, length us, event | category | flops | bytes accessed | tf_op | source)
XLA Modules:
  0.0 405.8 jit_solution(17831062169499786472)
XLA Ops:
  13.7 43.3 %collective-permute-done = bf16[1024,1024]{1,0:T(8,128)(2,1)} collective-permute-done((bf16[1024,1024]{1,0:T(8,128)(2,1)}, bf16[1024,1024]{1,0:T(8,128)(2,1)}, u32[]{:S(2)}, u32[]{:S(2)}) %collective-permute-start) | collective-permute-done | bytes 2097184 | tf_op jit(solution)/shard_map/ppermute | solution.py:19
  60.1 43.0 %collective-permute-done.1 = bf16[1024,1024]{1,0:T(8,128)(2,1)} collective-permute-done((bf16[1024,1024]{1,0:T(8,128)(2,1)}, bf16[1024,1024]{1,0:T(8,128)(2,1)}, u32[]{:S(2)}, u32[]{:S(2)}) %collective-permute-start.1) | collective-permute-done | bytes 2097184 | tf_op jit(solution)/shard_map/ppermute | solution.py:19
  111.0 34.9 %collective-permute-done.3 = bf16[1024,1024]{1,0:T(8,128)(2,1)S(1)} collective-permute-done((bf16[1024,1024]{1,0:T(8,128)(2,1)}, bf16[1024,1024]{1,0:T(8,128)(2,1)S(1)}, u32[]{:S(2)}, u32[]{:S(2)}) %collective-permute-start.3) | collective-permute-done | bytes 2097184 | tf_op jit(solution)/shard_map/ppermute | solution.py:19
  147.4 10.0 %fusion.45 = (f32[512]{0:T(512)S(1)}, bf16[512,5120]{1,0:T(8,128)(2,1)S(1)}) fusion(f32[5120]{0:T(1024)S(1)} %mul.152, bf16[5120,1024]{1,0:T(8,128)(2,1)} %constant_dynamic-update-slice_fusion, bf16[1024,1024]{1,0:T(8,128)(2,1)} %multiply_convert_fusion), kind=kOutput, calls=%fused_computation.114 | convolution fusion | flops 5384437248 | bytes 16799744 | tf_op jit(solution)/shard_map/dot_general | solution.py:92
  157.4 11.9 %fusion.44 = (f32[512]{0:T(512)S(1)}, bf16[512,5120]{1,0:T(8,128)(2,1)S(1)}) fusion(f32[5120]{0:T(1024)S(1)} %mul.158, bf16[5120,1024]{1,0:T(8,128)(2,1)} %constant_dynamic-update-slice_fusion, bf16[1024,1024]{1,0:T(8,128)(2,1)} %multiply_convert_fusion), kind=kOutput, calls=%fused_computation.113 | convolution fusion | flops 5384437248 | bytes 16799744 | tf_op jit(solution)/shard_map/dot_general | solution.py:92
  171.6 3.3 collective-permute-start.6
  174.8 10.5 %collective-permute-start.7 = (bf16[1024,64]{0,1:T(8,128)(2,1)S(1)}, bf16[1024,64]{0,1:T(8,128)(2,1)S(1)}, u32[]{:S(2)}, u32[]{:S(2)}) collective-permute-start(bf16[1024,64]{0,1:T(8,128)(2,1)S(1)} %multiply_convert_fusion.1), channel_id=1, source_target_pairs={{0,6},{1,7},{2,0},{3,1},{4,2},{5,3},{6,4},{7,5},{8,14},{9,15},{10,... | collective-permute-start | bytes 393224 | tf_op jit(solution)/shard_map/ppermute | solution.py:19
  192.9 34.8 %psum.42 = f32[64,64]{0,1:T(8,128)S(1)} all-reduce(f32[64,64]{0,1:T(8,128)S(1)} %fusion.9), channel_id=1, replica_groups=mesh['row'=4,'col'=8] {'col'}, use_global_device_ids=true, to_apply=%region_4.5 | all-reduce | flops 4096 | bytes 32768 | tf_op jit(solution)/shard_map/psum | solution.py:60
  227.7 10.3 %psum.43 = f32[64,64]{0,1:T(8,128)S(1)} all-reduce(f32[64,64]{0,1:T(8,128)S(1)} %psum.42), channel_id=1, replica_groups=mesh['row'=4,'col'=8] {'row'}, use_global_device_ids=true, to_apply=%region_5.6 | all-reduce | flops 4096 | bytes 32768 | tf_op jit(solution)/shard_map/psum | solution.py:60
  238.1 5.8 %cholesky.59 = f32[64,64]{1,0:T(8,128)S(1)} custom-call(f32[64,64]{1,0:T(8,128)S(1)} %fusion.18), custom_call_target="Cholesky" | custom-call | tf_op jit(solution)/shard_map/jit(cholesky)/cholesky | solution.py:61
  245.3 4.9 %custom-call.7 = f32[1,64,64]{1,2,0:T(8,128)S(1)} custom-call(f32[1,64,64]{2,1,0:T(8,128)S(1)} %fusion.10), custom_call_target="InvertDiagBlocksLowerTriangular" | custom-call | tf_op jit(solution)/shard_map/triangular_solve/custom-call.0 | solution.py:62
  250.7 4.7 %collective-permute-start.10 = (bf16[1024,64]{0,1:T(8,128)(2,1)S(1)}, bf16[1024,64]{0,1:T(8,128)(2,1)S(1)}, u32[]{:S(2)}, u32[]{:S(2)}) collective-permute-start(bf16[1024,64]{0,1:T(8,128)(2,1)S(1)} %fusion.3), channel_id=1, source_target_pairs={{0,7},{1,0},{2,1},{3,2},{4,3},{5,4},{6,5},{7,6},{8,15},{9,8},{10,9... | collective-permute-start | bytes 393224 | tf_op jit(solution)/shard_map/ppermute | solution.py:19
  261.3 4.2 %convolution_multiply_fusion.3 = f32[512,64]{0,1:T(8,128)S(1)} fusion(bf16[5120,64]{0,1:T(8,128)(2,1)S(1)} %constant_dynamic-update-slice_fusion.10, f32[512]{0:T(512)S(1)} %bitcast.68, bf16[512,5120]{1,0:T(8,128)(2,1)} %copy-done), kind=kOutput, calls=%fused_computation.15 | convolution fusion | flops 335577088 | bytes 6031360 | tf_op jit(solution)/shard_map/dot_general | solution.py:113
  267.6 36.1 %psum.44 = f32[64,64]{0,1:T(8,128)S(1)} all-reduce(f32[64,64]{0,1:T(8,128)S(1)} %fusion.8), channel_id=1, replica_groups=mesh['row'=4,'col'=8] {'col'}, use_global_device_ids=true, to_apply=%region_8.11 | all-reduce | flops 4096 | bytes 32768 | tf_op jit(solution)/shard_map/psum | solution.py:60
  303.7 10.3 %psum.45 = f32[64,64]{0,1:T(8,128)S(1)} all-reduce(f32[64,64]{0,1:T(8,128)S(1)} %psum.44), channel_id=1, replica_groups=mesh['row'=4,'col'=8] {'row'}, use_global_device_ids=true, to_apply=%region_9.12 | all-reduce | flops 4096 | bytes 32768 | tf_op jit(solution)/shard_map/psum | solution.py:60
  314.1 5.8 %cholesky.70 = f32[64,64]{1,0:T(8,128)S(1)} custom-call(f32[64,64]{1,0:T(8,128)S(1)} %fusion.16), custom_call_target="Cholesky" | custom-call | tf_op jit(solution)/shard_map/jit(cholesky)/cholesky | solution.py:61
  321.2 4.9 %custom-call.8 = f32[1,64,64]{1,2,0:T(8,128)S(1)} custom-call(f32[1,64,64]{2,1,0:T(8,128)S(1)} %fusion.11), custom_call_target="InvertDiagBlocksLowerTriangular" | custom-call | tf_op jit(solution)/shard_map/triangular_solve/custom-call.0 | solution.py:62
  326.7 4.7 %collective-permute-start.14 = (bf16[1024,64]{0,1:T(8,128)(2,1)S(1)}, bf16[1024,64]{0,1:T(8,128)(2,1)S(1)}, u32[]{:S(2)}, u32[]{:S(2)}) collective-permute-start(bf16[1024,64]{0,1:T(8,128)(2,1)S(1)} %fusion.4), channel_id=1, source_target_pairs={{0,7},{1,0},{2,1},{3,2},{4,3},{5,4},{6,5},{7,6},{8,15},{9,8},{10,9... | collective-permute-start | bytes 393224 | tf_op jit(solution)/shard_map/ppermute | solution.py:19
  337.3 4.2 %convolution_multiply_fusion.1 = f32[512,64]{0,1:T(8,128)S(1)} fusion(bf16[5120,64]{0,1:T(8,128)(2,1)S(1)} %constant_dynamic-update-slice_fusion.15, f32[512]{0:T(512)S(1)} %bitcast.69, bf16[512,5120]{1,0:T(8,128)(2,1)} %copy-done), kind=kOutput, calls=%fused_computation.13 | convolution fusion | flops 335577088 | bytes 6031360 | tf_op jit(solution)/shard_map/dot_general | solution.py:113
  341.5 4.2 %convolution_multiply_fusion = f32[512,64]{0,1:T(8,128)S(1)} fusion(bf16[5120,64]{0,1:T(8,128)(2,1)S(1)} %constant_dynamic-update-slice_fusion.15, f32[512]{0:T(512)S(1)} %bitcast.66, bf16[512,5120]{1,0:T(8,128)(2,1)} %copy-done.1), kind=kOutput, calls=%fused_computation.12 | convolution fusion | flops 335577088 | bytes 6031360 | tf_op jit(solution)/shard_map/dot_general | solution.py:113
  346.0 36.2 %psum.46 = f32[64,64]{0,1:T(8,128)S(1)} all-reduce(f32[64,64]{0,1:T(8,128)S(1)} %fusion.7), channel_id=1, replica_groups=mesh['row'=4,'col'=8] {'col'}, use_global_device_ids=true, to_apply=%region_10.13 | all-reduce | flops 4096 | bytes 32768 | tf_op jit(solution)/shard_map/psum | solution.py:60
  382.2 10.3 %psum.47 = f32[64,64]{0,1:T(8,128)S(1)} all-reduce(f32[64,64]{0,1:T(8,128)S(1)} %psum.46), channel_id=1, replica_groups=mesh['row'=4,'col'=8] {'row'}, use_global_device_ids=true, to_apply=%region_11.14 | all-reduce | flops 4096 | bytes 32768 | tf_op jit(solution)/shard_map/psum | solution.py:60
  392.6 5.8 %cholesky.81 = f32[64,64]{1,0:T(8,128)S(1)} custom-call(f32[64,64]{1,0:T(8,128)S(1)} %fusion.14), custom_call_target="Cholesky" | custom-call | tf_op jit(solution)/shard_map/jit(cholesky)/cholesky | solution.py:61
  399.7 4.9 %custom-call.9 = f32[1,64,64]{1,2,0:T(8,128)S(1)} custom-call(f32[1,64,64]{2,1,0:T(8,128)S(1)} %fusion.12), custom_call_target="InvertDiagBlocksLowerTriangular" | custom-call | tf_op jit(solution)/shard_map/triangular_solve/custom-call.0 | solution.py:62
  (101 shorter events, 56.3 us)
Async XLA Ops:
  0.0 3.4 copy-start.3
  0.0 13.1 %copy-start.6 = (s32[2,12]{1,0:T(2,128)S(1)}, s32[2,12]{1,0:T(2,128)}, u32[]{:S(2)}) copy-start(s32[2,12]{1,0:T(2,128)} %param.7) | copy-start | bytes 292
  5.1 51.9 %collective-permute-start = (bf16[1024,1024]{1,0:T(8,128)(2,1)}, bf16[1024,1024]{1,0:T(8,128)(2,1)}, u32[]{:S(2)}, u32[]{:S(2)}) collective-permute-start(bf16[1024,1024]{1,0:T(8,128)(2,1)} %multiply_convert_fusion), channel_id=1, source_target_pairs={{0,2},{1,3},{2,4},{3,5},{4,6},{5,7},{6,0},{7,1},{8,10},{9,11},{10,... | collective-permute-start | bytes 6291464 | tf_op jit(solution)/shard_map/ppermute | solution.py:19
  8.1 94.9 %collective-permute-start.1 = (bf16[1024,1024]{1,0:T(8,128)(2,1)}, bf16[1024,1024]{1,0:T(8,128)(2,1)}, u32[]{:S(2)}, u32[]{:S(2)}) collective-permute-start(bf16[1024,1024]{1,0:T(8,128)(2,1)} %multiply_convert_fusion), channel_id=1, source_target_pairs={{0,1},{1,2},{2,3},{3,4},{4,5},{5,6},{6,7},{7,0},{8,9},{9,10},{10,1... | collective-permute-start | bytes 6291464 | tf_op jit(solution)/shard_map/ppermute | solution.py:19
  9.6 98.2 %collective-permute-start.2 = (bf16[1024,1024]{1,0:T(8,128)(2,1)}, bf16[1024,1024]{1,0:T(8,128)(2,1)}, u32[]{:S(2)}, u32[]{:S(2)}) collective-permute-start(bf16[1024,1024]{1,0:T(8,128)(2,1)} %multiply_convert_fusion), channel_id=1, source_target_pairs={{0,7},{1,0},{2,1},{3,2},{4,3},{5,4},{6,5},{7,6},{8,15},{9,8},{10,9... | collective-permute-start | bytes 6291464 | tf_op jit(solution)/shard_map/ppermute | solution.py:19
  12.9 133.0 %collective-permute-start.3 = (bf16[1024,1024]{1,0:T(8,128)(2,1)}, bf16[1024,1024]{1,0:T(8,128)(2,1)S(1)}, u32[]{:S(2)}, u32[]{:S(2)}) collective-permute-start(bf16[1024,1024]{1,0:T(8,128)(2,1)} %multiply_convert_fusion), channel_id=1, source_target_pairs={{0,6},{1,7},{2,0},{3,1},{4,2},{5,3},{6,4},{7,5},{8,14},{9,15},{10,... | collective-permute-start | bytes 6291464 | tf_op jit(solution)/shard_map/ppermute | solution.py:19
  13.7 92.5 %copy-start.4 = (f32[1024,1024]{1,0:T(8,128)S(1)}, f32[1024,1024]{1,0:T(8,128)}, u32[]{:S(2)}) copy-start(f32[1024,1024]{1,0:T(8,128)} %param.6) | copy-start | bytes 12582916
  157.4 31.7 %copy-start = (bf16[512,5120]{1,0:T(8,128)(2,1)}, bf16[512,5120]{1,0:T(8,128)(2,1)S(1)}, u32[]{:S(2)}) copy-start(bf16[512,5120]{1,0:T(8,128)(2,1)S(1)} %get-tuple-element.16) | copy-start | bytes 15728644
  157.4 12.0 %copy-start.5 = (f32[1024,64]{0,1:T(8,128)S(1)}, f32[1024,64]{0,1:T(8,128)}, u32[]{:S(2)}) copy-start(f32[1024,64]{0,1:T(8,128)} %param.8) | copy-start | bytes 786436
  169.4 23.2 %copy-start.1 = (bf16[512,5120]{1,0:T(8,128)(2,1)}, bf16[512,5120]{1,0:T(8,128)(2,1)S(1)}, u32[]{:S(2)}) copy-start(bf16[512,5120]{1,0:T(8,128)(2,1)S(1)} %get-tuple-element.14) | copy-start | bytes 15728644
  169.4 15.8 %collective-permute-start.4 = (bf16[1024,64]{0,1:T(8,128)(2,1)S(1)}, bf16[1024,64]{0,1:T(8,128)(2,1)S(1)}, u32[]{:S(2)}, u32[]{:S(2)}) collective-permute-start(bf16[1024,64]{0,1:T(8,128)(2,1)S(1)} %multiply_convert_fusion.1), channel_id=1, source_target_pairs={{0,2},{1,3},{2,4},{3,5},{4,6},{5,7},{6,0},{7,1},{8,10},{9,11},{10,... | collective-permute-start | bytes 393224 | tf_op jit(solution)/shard_map/ppermute | solution.py:19
  170.1 15.2 %collective-permute-start.5 = (bf16[1024,64]{0,1:T(8,128)(2,1)S(1)}, bf16[1024,64]{0,1:T(8,128)(2,1)S(1)}, u32[]{:S(2)}, u32[]{:S(2)}) collective-permute-start(bf16[1024,64]{0,1:T(8,128)(2,1)S(1)} %multiply_convert_fusion.1), channel_id=1, source_target_pairs={{0,1},{1,2},{2,3},{3,4},{4,5},{5,6},{6,7},{7,0},{8,9},{9,10},{10,1... | collective-permute-start | bytes 393224 | tf_op jit(solution)/shard_map/ppermute | solution.py:19
  171.6 14.7 %collective-permute-start.6 = (bf16[1024,64]{0,1:T(8,128)(2,1)S(1)}, bf16[1024,64]{0,1:T(8,128)(2,1)S(1)}, u32[]{:S(2)}, u32[]{:S(2)}) collective-permute-start(bf16[1024,64]{0,1:T(8,128)(2,1)S(1)} %multiply_convert_fusion.1), channel_id=1, source_target_pairs={{0,7},{1,0},{2,1},{3,2},{4,3},{5,4},{6,5},{7,6},{8,15},{9,8},{10,9... | collective-permute-start | bytes 393224 | tf_op jit(solution)/shard_map/ppermute | solution.py:19
  174.8 14.3 %collective-permute-start.7 = (bf16[1024,64]{0,1:T(8,128)(2,1)S(1)}, bf16[1024,64]{0,1:T(8,128)(2,1)S(1)}, u32[]{:S(2)}, u32[]{:S(2)}) collective-permute-start(bf16[1024,64]{0,1:T(8,128)(2,1)S(1)} %multiply_convert_fusion.1), channel_id=1, source_target_pairs={{0,6},{1,7},{2,0},{3,1},{4,2},{5,3},{6,4},{7,5},{8,14},{9,15},{10,... | collective-permute-start | bytes 393224 | tf_op jit(solution)/shard_map/ppermute | solution.py:19
  250.2 15.3 %copy-start.2 = (bf16[512,5120]{1,0:T(8,128)(2,1)S(1)}, bf16[512,5120]{1,0:T(8,128)(2,1)}, u32[]{:S(2)}) copy-start(bf16[512,5120]{1,0:T(8,128)(2,1)} %copy-done.1) | copy-start | bytes 15728644
  250.6 7.9 %collective-permute-start.8 = (bf16[1024,64]{0,1:T(8,128)(2,1)S(1)}, bf16[1024,64]{0,1:T(8,128)(2,1)S(1)}, u32[]{:S(2)}, u32[]{:S(2)}) collective-permute-start(bf16[1024,64]{0,1:T(8,128)(2,1)S(1)} %fusion.3), channel_id=1, source_target_pairs={{0,2},{1,3},{2,4},{3,5},{4,6},{5,7},{6,0},{7,1},{8,10},{9,11},{10,... | collective-permute-start | bytes 393224 | tf_op jit(solution)/shard_map/ppermute | solution.py:19
  250.7 9.2 %collective-permute-start.9 = (bf16[1024,64]{0,1:T(8,128)(2,1)S(1)}, bf16[1024,64]{0,1:T(8,128)(2,1)S(1)}, u32[]{:S(2)}, u32[]{:S(2)}) collective-permute-start(bf16[1024,64]{0,1:T(8,128)(2,1)S(1)} %fusion.3), channel_id=1, source_target_pairs={{0,1},{1,2},{2,3},{3,4},{4,5},{5,6},{6,7},{7,0},{8,9},{9,10},{10,1... | collective-permute-start | bytes 393224 | tf_op jit(solution)/shard_map/ppermute | solution.py:19
  250.7 9.1 %collective-permute-start.10 = (bf16[1024,64]{0,1:T(8,128)(2,1)S(1)}, bf16[1024,64]{0,1:T(8,128)(2,1)S(1)}, u32[]{:S(2)}, u32[]{:S(2)}) collective-permute-start(bf16[1024,64]{0,1:T(8,128)(2,1)S(1)} %fusion.3), channel_id=1, source_target_pairs={{0,7},{1,0},{2,1},{3,2},{4,3},{5,4},{6,5},{7,6},{8,15},{9,8},{10,9... | collective-permute-start | bytes 393224 | tf_op jit(solution)/shard_map/ppermute | solution.py:19
  255.4 5.8 %collective-permute-start.11 = (bf16[1024,64]{0,1:T(8,128)(2,1)S(1)}, bf16[1024,64]{0,1:T(8,128)(2,1)S(1)}, u32[]{:S(2)}, u32[]{:S(2)}) collective-permute-start(bf16[1024,64]{0,1:T(8,128)(2,1)S(1)} %fusion.3), channel_id=1, source_target_pairs={{0,6},{1,7},{2,0},{3,1},{4,2},{5,3},{6,4},{7,5},{8,14},{9,15},{10,... | collective-permute-start | bytes 393224 | tf_op jit(solution)/shard_map/ppermute | solution.py:19
  326.6 7.9 %collective-permute-start.12 = (bf16[1024,64]{0,1:T(8,128)(2,1)S(1)}, bf16[1024,64]{0,1:T(8,128)(2,1)S(1)}, u32[]{:S(2)}, u32[]{:S(2)}) collective-permute-start(bf16[1024,64]{0,1:T(8,128)(2,1)S(1)} %fusion.4), channel_id=1, source_target_pairs={{0,2},{1,3},{2,4},{3,5},{4,6},{5,7},{6,0},{7,1},{8,10},{9,11},{10,... | collective-permute-start | bytes 393224 | tf_op jit(solution)/shard_map/ppermute | solution.py:19
  326.6 9.1 %collective-permute-start.13 = (bf16[1024,64]{0,1:T(8,128)(2,1)S(1)}, bf16[1024,64]{0,1:T(8,128)(2,1)S(1)}, u32[]{:S(2)}, u32[]{:S(2)}) collective-permute-start(bf16[1024,64]{0,1:T(8,128)(2,1)S(1)} %fusion.4), channel_id=1, source_target_pairs={{0,1},{1,2},{2,3},{3,4},{4,5},{5,6},{6,7},{7,0},{8,9},{9,10},{10,1... | collective-permute-start | bytes 393224 | tf_op jit(solution)/shard_map/ppermute | solution.py:19
  326.7 9.1 %collective-permute-start.14 = (bf16[1024,64]{0,1:T(8,128)(2,1)S(1)}, bf16[1024,64]{0,1:T(8,128)(2,1)S(1)}, u32[]{:S(2)}, u32[]{:S(2)}) collective-permute-start(bf16[1024,64]{0,1:T(8,128)(2,1)S(1)} %fusion.4), channel_id=1, source_target_pairs={{0,7},{1,0},{2,1},{3,2},{4,3},{5,4},{6,5},{7,6},{8,15},{9,8},{10,9... | collective-permute-start | bytes 393224 | tf_op jit(solution)/shard_map/ppermute | solution.py:19
  331.4 5.8 %collective-permute-start.15 = (bf16[1024,64]{0,1:T(8,128)(2,1)S(1)}, bf16[1024,64]{0,1:T(8,128)(2,1)S(1)}, u32[]{:S(2)}, u32[]{:S(2)}) collective-permute-start(bf16[1024,64]{0,1:T(8,128)(2,1)S(1)} %fusion.4), channel_id=1, source_target_pairs={{0,6},{1,7},{2,0},{3,1},{4,2},{5,3},{6,4},{7,5},{8,14},{9,15},{10,... | collective-permute-start | bytes 393224 | tf_op jit(solution)/shard_map/ppermute | solution.py:19
